TPU v7x, 32 devices: a whole 2x2x4 slice. The times are simulated.
32 devices in a mesh: pipe: 2 (over x), expert: 16 (over z, y, core).
Axes of the slice: x: 2, y: 2, z: 4, core: 2. Of those that a mesh axis runs over, the one named last changes fastest.
Arguments:
- front_tokens: bfloat16 [2, 192, 3584], P('pipe', 'expert'), may hold values from -6 to 6
- front_routes: int32 [2, 192, 2], P('pipe', 'expert'), may hold values from 0 to 1, all different within a row; in each aligned block of 12 rows (0 to 11, 12 to 23, ..., all dimensions but the last counted through in order) at most 12 rows name the same one
- front_mixing: int32 [2, 192, 2], P('pipe', 'expert'), may hold values from 1 to 15
- back_tokens: bfloat16 [2, 192, 3584], P('pipe', 'expert'), may hold values from -6 to 6
- back_routes: int32 [2, 192, 2], P('pipe', 'expert'), may hold values from 0 to 1, all different within a row; in each aligned block of 12 rows (0 to 11, 12 to 23, ..., all dimensions but the last counted through in order) at most 12 rows name the same one
- back_mixing: int32 [2, 192, 2], P('pipe', 'expert'), may hold values from 1 to 15
- back_upstream: bfloat16 [2, 192, 3584], P('pipe', 'expert'), may hold values from -6 to 6
- gate_weight: bfloat16 [2, 3584, 2048], P('pipe', None, 'expert'), may hold values from -0.09375 to 0.09375
- up_weight: bfloat16 [2, 3584, 2048], P('pipe', None, 'expert'), may hold values from -0.09375 to 0.09375
- down_weight: bfloat16 [2, 2048, 3584], P('pipe', 'expert'), may hold values from -0.1875 to 0.1875
Outputs:
- front_result: bfloat16 [2, 192, 3584], P('pipe', 'expert')
- token_grads: bfloat16 [2, 192, 3584], P('pipe', 'expert')
- gate_grads: bfloat16 [2, 1792, 2048], P('pipe', None, 'expert')
- up_grads: bfloat16 [2, 1792, 2048], P('pipe', None, 'expert')
- down_grads: bfloat16 [2, 2048, 1792], P('pipe', 'expert')
Inputs may be any that keep to these rules, and one draw needn't show every extreme that they name: `front_routes`: each row names 2 different experts; within each device's block of 12 rows no expert is named more than 12 times, a bound that some block reaches. `back_routes`: each row names 2 different experts; within each device's block of 12 rows no expert is named more than 12 times, a bound that some block reaches.
All inputs are finite; a program needn't handle non-finite values.
Results may differ from a plain program's by a relative error of at most 0.0071.
Values may be sent and summed in bfloat16 or wider, within the bound.
A program may use at most 64 MiB of HBM per device.

v0:
```python
import jax
import jax.numpy as jnp
from jax import lax
from jax.sharding import PartitionSpec as P

SHARDS = 8
weight_unit = 0.0625


def hit_tables(routes, mixing, experts, capacity):
    token_count, route_count = routes.shape
    flat_routes = routes.reshape(token_count * route_count)
    matches = (flat_routes[:, None] == jnp.arange(experts, dtype=jnp.int32)[None, :]).astype(
        jnp.int32
    )
    earlier = jnp.cumsum(matches, axis=0) - matches
    position = jnp.sum(earlier * matches, axis=1)
    slot_ids = flat_routes * capacity + position
    hit_table = (
        slot_ids[:, None] == jnp.arange(experts * capacity, dtype=jnp.int32)[None, :]
    ).astype(jnp.float32)
    hit_table = hit_table.reshape(token_count, route_count, experts * capacity)
    weights = mixing.astype(jnp.float32) * weight_unit
    picker = jnp.sum(hit_table, axis=1)
    mix_table = jnp.sum(hit_table * weights[:, :, None], axis=1)
    return (picker, mix_table)


def deliver(slot_rows, experts, capacity):
    stacks = slot_rows.shape[0]
    feature_count = slot_rows.shape[2]
    copies = jnp.repeat(slot_rows.reshape(stacks, experts, capacity, feature_count), SHARDS, axis=1)
    landed = lax.all_to_all(copies, "expert", split_axis=1, concat_axis=1, tiled=True)
    return landed.reshape(stacks, experts * SHARDS * capacity, feature_count)


def collect(shard_parts, experts, capacity):
    feature_count = shard_parts.shape[1]
    sources = experts * SHARDS
    returned = lax.all_to_all(
        shard_parts.reshape(sources, capacity, feature_count),
        "expert",
        split_axis=0,
        concat_axis=0,
        tiled=True,
    )
    summed = jnp.sum(
        returned.reshape(experts, SHARDS, capacity, feature_count).astype(jnp.float32), axis=1
    )
    result_rows = summed.astype(jnp.bfloat16).reshape(experts * capacity, feature_count)
    return result_rows


def mirror_move(values, split_dim, concat_dim):
    return lax.all_to_all(values, "pipe", split_axis=split_dim, concat_axis=concat_dim, tiled=True)


def local(
    front_tokens,
    front_routes,
    front_mixing,
    back_tokens,
    back_routes,
    back_mixing,
    back_upstream,
    gate_weight,
    up_weight,
    down_weight,
):
    experts = lax.axis_size("expert") // SHARDS
    token_count = front_tokens.shape[1]
    route_count = front_routes.shape[2]
    feature_count = front_tokens.shape[2]
    capacity = min(token_count, max(2, 3 * token_count * route_count // (2 * experts)))
    front_pick, front_mix = hit_tables(front_routes[0], front_mixing[0], experts, capacity)
    back_pick, back_mix = hit_tables(back_routes[0], back_mixing[0], experts, capacity)
    front_slots = jnp.dot(
        front_pick.T.astype(jnp.bfloat16), front_tokens[0], preferred_element_type=jnp.float32
    ).astype(jnp.bfloat16)
    back_slots = jnp.dot(
        back_pick.T.astype(jnp.bfloat16), back_tokens[0], preferred_element_type=jnp.float32
    ).astype(jnp.bfloat16)
    scaled_slots = jnp.dot(
        back_mix.T, back_upstream[0].astype(jnp.float32), precision=lax.Precision.HIGHEST
    ).astype(jnp.bfloat16)
    landed = deliver(jnp.stack([front_slots, back_slots, scaled_slots]), experts, capacity)
    gate_cols = gate_weight[0]
    up_cols = up_weight[0]
    down_rows = down_weight[0]
    front_rows = landed[0]
    front_gate = jnp.dot(front_rows, gate_cols, preferred_element_type=jnp.float32)
    front_up = jnp.dot(front_rows, up_cols, preferred_element_type=jnp.float32)
    front_hidden = (jax.nn.silu(front_gate) * front_up).astype(jnp.bfloat16)
    front_parts = jnp.dot(front_hidden, down_rows, preferred_element_type=jnp.float32).astype(
        jnp.bfloat16
    )
    front_summed = collect(front_parts, experts, capacity)
    front_result = jnp.dot(
        front_mix, front_summed.astype(jnp.float32), precision=lax.Precision.HIGHEST
    ).astype(jnp.bfloat16)
    back_rows = landed[1]
    scaled_rows = landed[2]
    back_gate = jnp.dot(back_rows, gate_cols, preferred_element_type=jnp.float32)
    back_up = jnp.dot(back_rows, up_cols, preferred_element_type=jnp.float32)
    gate_act = jax.nn.silu(back_gate)
    gate_sig = jax.nn.sigmoid(back_gate)
    back_hidden = (gate_act * back_up).astype(jnp.bfloat16)
    down_section = jnp.dot(scaled_rows.T, back_hidden, preferred_element_type=jnp.float32).astype(
        jnp.bfloat16
    )
    hidden_grad = jnp.dot(scaled_rows, down_rows.T, preferred_element_type=jnp.float32)
    act_slope = gate_sig * (1.0 + back_gate * (1.0 - gate_sig))
    gate_delta = (hidden_grad * back_up * act_slope).astype(jnp.bfloat16)
    up_delta = (hidden_grad * gate_act).astype(jnp.bfloat16)
    gate_section = jnp.dot(back_rows.T, gate_delta, preferred_element_type=jnp.float32).astype(
        jnp.bfloat16
    )
    up_section = jnp.dot(back_rows.T, up_delta, preferred_element_type=jnp.float32).astype(
        jnp.bfloat16
    )
    back_parts = (
        jnp.dot(gate_delta, gate_cols.T, preferred_element_type=jnp.float32)
        + jnp.dot(up_delta, up_cols.T, preferred_element_type=jnp.float32)
    ).astype(jnp.bfloat16)
    grad_slots = collect(back_parts, experts, capacity)
    token_grads = jnp.dot(
        back_pick.astype(jnp.bfloat16), grad_slots, preferred_element_type=jnp.float32
    ).astype(jnp.bfloat16)
    section_grads = lax.optimization_barrier(jnp.stack([gate_section, up_section, down_section]))
    pipe_count = lax.axis_size("pipe")
    half_rows = feature_count // 2
    upper_half = lax.axis_index("pipe") * 2 >= pipe_count
    own_half = jnp.where(upper_half, section_grads[:, half_rows:], section_grads[:, :half_rows])
    leaving = jnp.where(upper_half, section_grads[:, :half_rows], section_grads[:, half_rows:])
    piece_rows = half_rows // pipe_count
    spread_out = mirror_move(leaving, 1, 0)
    by_source = spread_out.reshape(pipe_count, 3, piece_rows, leaving.shape[2])
    reversed_sources = jnp.flip(by_source, axis=0).reshape(
        pipe_count * 3, piece_rows, leaving.shape[2]
    )
    leaving = mirror_move(reversed_sources, 0, 1)
    summed = (own_half.astype(jnp.float32) + leaving.astype(jnp.float32)).astype(jnp.bfloat16)
    return (
        front_result[None],
        token_grads[None],
        summed[0][None],
        summed[1][None],
        summed[2].T[None],
    )


def solution(mesh):
    placed = (
        P("pipe", "expert", None),
        P("pipe", "expert", None),
        P("pipe", "expert", None),
        P("pipe", "expert", None),
        P("pipe", "expert", None),
        P("pipe", "expert", None),
        P("pipe", "expert", None),
        P("pipe", None, "expert"),
        P("pipe", None, "expert"),
        P("pipe", "expert", None),
    )
    return jax.shard_map(
        local,
        mesh=mesh,
        in_specs=placed,
        out_specs=(
            P("pipe", "expert", None),
            P("pipe", "expert", None),
            P("pipe", None, "expert"),
            P("pipe", None, "expert"),
            P("pipe", "expert", None),
        ),
        check_vma=False,
    )
```

profile of v0, /device:TPU:13, one launch (start us, length us, event | category | flops | bytes accessed | tf_op | source)
XLA Modules:
  0.0 313.1 jit_solution(14618682792077326766)
XLA Ops:
  0.7 0.9 copy.61
  1.5 0.1 eq.58
  1.7 0.2 select_reduce_fusion.3
  2.0 0.1 copy.62
  2.1 0.7 bitcast_add_fusion.2
  2.8 0.1 copy.63
  2.9 0.7 multiply_bitcast_fusion.1
  3.6 0.1 copy.64
  3.7 0.8 copy.65
  4.6 0.2 select_reduce_fusion.1
  4.9 0.1 copy.66
  5.0 0.7 bitcast_add_fusion.1
  5.7 0.1 copy.67
  5.8 0.7 multiply_bitcast_fusion
  6.5 0.1 copy.68
  6.6 0.1 convert_reduce_fusion
  6.7 1.2 convolution_convert_fusion.4
  8.0 1.1 convolution_convert_fusion.5
  9.2 0.1 convert_reduce_fusion.1
  9.3 0.2 convolution_convert_fusion.6
  9.6 0.1 pad_maximum_fusion.1
  9.8 3.1 broadcast_in_dim.8
  12.9 6.6 %all-to-all-start = ((bf16[3,16,12,3584]{3,2,0,1:T(8,128)(2,1)}), bf16[3,16,12,3584]{3,2,0,1:T(8,128)(2,1)}, u32[]{:S(2)}, u32[]{:S(2)}) async-start(bf16[3,16,12,3584]{3,2,0,1:T(8,128)(2,1)} %bitcast.97), calls=%async_computation | async-start | bytes 11010048 | tf_op jit(solution)/shard_map/all_to_all | solution.py:33
  19.4 120.6 %all-to-all-done = bf16[3,16,12,3584]{3,2,0,1:T(8,128)(2,1)} async-done(((bf16[3,16,12,3584]{3,2,0,1:T(8,128)(2,1)}), bf16[3,16,12,3584]{3,2,0,1:T(8,128)(2,1)}, u32[]{:S(2)}, u32[]{:S(2)}) %all-to-all-start) | async-done | bytes 4128800 | tf_op jit(solution)/shard_map/all_to_all | solution.py:33
  140.0 5.2 %fusion.40 = (bf16[1,16,12,3584]{3,2,0,1:T(8,128)(2,1)}, bf16[1,16,12,3584]{3,2,0,1:T(8,128)(2,1)}, bf16[1,16,12,3584]{3,2,0,1:T(8,128)(2,1)}) fusion(bf16[3,16,12,3584]{3,2,0,1:T(8,128)(2,1)} %all-to-all-done), kind=kLoop, calls=%fused_computation.75 | loop fusion | bytes 8257536 | tf_op jit(solution)/shard_map/slice | solution.py:102
  145.2 2.4 squeeze.40
  147.6 0.5 fusion.18
  148.1 0.5 fusion.12
  148.7 3.4 %squeeze.39 = bf16[192,3584]{1,0:T(8,128)(2,1)} reshape(bf16[1,16,12,3584]{3,2,0,1:T(8,128)(2,1)} %get-tuple-element.34) | data formatting | bytes 2752512 | tf_op jit(solution)/shard_map/squeeze | solution.py:102
  152.1 2.2 fusion.3
  154.3 0.5 multiply_convert_fusion.1
  154.8 0.7 fusion.2
  155.5 0.7 fusion.1
  156.3 0.3 pad_maximum_fusion
  156.6 0.1 broadcast_select_fusion
  156.7 1.4 copy-done.1
  158.1 8.5 %copy.70 = bf16[3,1792,128]{2,0,1:T(4,128)(2,1)S(1)} copy(bf16[3,1792,128]{2,1,0:T(8,128)(2,1)S(1)} %broadcast_select_fusion) | data formatting | bytes 2752512 | tf_op jit(solution)/shard_map/jit(_where)/select_n | solution.py:134
  166.6 24.4 %all_to_all.39 = bf16[3,1792,128]{2,0,1:T(4,128)(2,1)S(1)} all-to-all(bf16[3,1792,128]{2,0,1:T(4,128)(2,1)S(1)} %copy.70), channel_id=1, replica_groups=mesh['pipe'=2,'expert'=16] {'pipe'}, dimensions={1} | all-to-all | bytes 2752512 | tf_op jit(solution)/shard_map/all_to_all | solution.py:55
  191.1 0.2 copy.71
  191.3 1.2 reverse.3
  192.5 2.5 copy.72
  195.0 4.8 %all-to-all-start.4 = ((bf16[6,896,128]{2,1,0:T(8,128)(2,1)}), bf16[6,896,128]{2,1,0:T(8,128)(2,1)}, u32[]{:S(2)}, u32[]{:S(2)}) async-start(bf16[6,896,128]{2,1,0:T(8,128)(2,1)} %bitcast.20), calls=%async_computation.4 | async-start | bytes 2752512 | tf_op jit(solution)/shard_map/all_to_all | solution.py:55
  199.7 2.4 squeeze.35
  202.1 0.5 fusion.20
  202.6 3.2 %convolution_convert_fusion = bf16[192,3584]{1,0:T(8,128)(2,1)} fusion(bf16[192,3584]{1,0:T(8,128)(2,1)S(1)} %squeeze.35, bf16[1,128,3584]{2,1,0:T(8,128)(2,1)} %param.19, bf16[1,3584,128]{2,1,0:T(8,128)(2,1)S(1)} %copy-done, f32[192,128]{1,0:T(8,128)S(1)} %fusion.20), kind=kOutput, calls=%fused_computation.2 | convolution fusion | flops 353157120 | bytes 4685824 | tf_op jit(solution)/shard_map/dot_general | solution.py:94
  205.9 3.3 %reshape.117 = bf16[16,12,3584]{2,1,0:T(8,128)(2,1)} reshape(bf16[192,3584]{1,0:T(8,128)(2,1)} %convolution_convert_fusion) | data formatting | bytes 2752512 | tf_op jit(solution)/shard_map/reshape | solution.py:41
  209.1 6.6 %all-to-all-done.4 = bf16[6,896,128]{2,1,0:T(8,128)(2,1)} async-done(((bf16[6,896,128]{2,1,0:T(8,128)(2,1)}), bf16[6,896,128]{2,1,0:T(8,128)(2,1)}, u32[]{:S(2)}, u32[]{:S(2)}) %all-to-all-start.4) | async-done | bytes 1376288 | tf_op jit(solution)/shard_map/all_to_all | solution.py:55
  215.7 6.7 %all-to-all-start.1 = ((bf16[16,12,3584]{2,1,0:T(8,128)(2,1)}), bf16[16,12,3584]{2,1,0:T(8,128)(2,1)}, u32[]{:S(2)}, u32[]{:S(2)}) async-start(bf16[16,12,3584]{2,1,0:T(8,128)(2,1)} %reshape.117), calls=%async_computation.1 | async-start | bytes 3670016 | tf_op jit(solution)/shard_map/all_to_all | solution.py:40
  222.4 0.5 fusion.16
  222.9 0.5 fusion
  223.5 1.4 reshape.120
  224.9 39.4 %all-to-all-done.1 = bf16[16,12,3584]{2,1,0:T(8,128)(2,1)} async-done(((bf16[16,12,3584]{2,1,0:T(8,128)(2,1)}), bf16[16,12,3584]{2,1,0:T(8,128)(2,1)}, u32[]{:S(2)}, u32[]{:S(2)}) %all-to-all-start.1) | async-done | bytes 1376288 | tf_op jit(solution)/shard_map/all_to_all | solution.py:40
  264.3 4.9 %all-to-all-start.2 = ((bf16[16,12,3584]{2,1,0:T(8,128)(2,1)}), bf16[16,12,3584]{2,1,0:T(8,128)(2,1)S(1)}, u32[]{:S(2)}, u32[]{:S(2)}) async-start(bf16[16,12,3584]{2,1,0:T(8,128)(2,1)} %reshape.120), calls=%async_computation.2 | async-start | bytes 3670016 | tf_op jit(solution)/shard_map/all_to_all | solution.py:40
  269.2 1.5 convert_bitcast_fusion
  270.8 0.2 copy.73
  271.0 1.6 copy-done.2
  272.5 0.4 fusion.6
  273.0 1.0 slice_bitcast_fusion
  274.0 1.0 copy.74
  275.0 1.8 bitcast_reduce_fusion.1
  276.8 34.2 %all-to-all-done.2 = bf16[16,12,3584]{2,1,0:T(8,128)(2,1)S(1)} async-done(((bf16[16,12,3584]{2,1,0:T(8,128)(2,1)}), bf16[16,12,3584]{2,1,0:T(8,128)(2,1)S(1)}, u32[]{:S(2)}, u32[]{:S(2)}) %all-to-all-start.2) | async-done | bytes 1376288 | tf_op jit(solution)/shard_map/all_to_all | solution.py:40
  311.0 0.3 bitcast_reduce_fusion
  311.4 0.8 fusion.5
  312.2 0.9 fusion.4
  (25 shorter events, 0.8 us)
Async XLA Ops:
  0.6 147.5 %copy-start = (bf16[1,3584,128]{2,1,0:T(8,128)(2,1)S(1)}, bf16[1,3584,128]{2,1,0:T(8,128)(2,1)}, u32[]{:S(2)}) copy-start(bf16[1,3584,128]{2,1,0:T(8,128)(2,1)} %param.18) | copy-start | bytes 2752516
  0.6 8.7 %copy-start.6 = (bf16[1,12,3584]{2,1,0:T(8,128)(2,1)S(1)}, bf16[1,12,3584]{2,1,0:T(8,128)(2,1)}, u32[]{:S(2)}) copy-start(bf16[1,12,3584]{2,1,0:T(8,128)(2,1)} %param.10) | copy-start | bytes 258052
  12.9 127.1 %all-to-all-start = ((bf16[3,16,12,3584]{3,2,0,1:T(8,128)(2,1)}), bf16[3,16,12,3584]{3,2,0,1:T(8,128)(2,1)}, u32[]{:S(2)}, u32[]{:S(2)}) async-start(bf16[3,16,12,3584]{3,2,0,1:T(8,128)(2,1)} %bitcast.97), calls=%async_computation | async-start | bytes 11010048 | tf_op jit(solution)/shard_map/all_to_all | solution.py:33
  145.2 2.5 copy-start.3
  152.1 2.2 copy-start.4
  152.1 2.2 copy-start.5
  156.6 1.6 copy-start.1
  195.0 20.8 %all-to-all-start.4 = ((bf16[6,896,128]{2,1,0:T(8,128)(2,1)}), bf16[6,896,128]{2,1,0:T(8,128)(2,1)}, u32[]{:S(2)}, u32[]{:S(2)}) async-start(bf16[6,896,128]{2,1,0:T(8,128)(2,1)} %bitcast.20), calls=%async_computation.4 | async-start | bytes 2752512 | tf_op jit(solution)/shard_map/all_to_all | solution.py:55
  215.7 48.6 %all-to-all-start.1 = ((bf16[16,12,3584]{2,1,0:T(8,128)(2,1)}), bf16[16,12,3584]{2,1,0:T(8,128)(2,1)}, u32[]{:S(2)}, u32[]{:S(2)}) async-start(bf16[16,12,3584]{2,1,0:T(8,128)(2,1)} %reshape.117), calls=%async_computation.1 | async-start | bytes 3670016 | tf_op jit(solution)/shard_map/all_to_all | solution.py:40
  264.3 46.7 %all-to-all-start.2 = ((bf16[16,12,3584]{2,1,0:T(8,128)(2,1)}), bf16[16,12,3584]{2,1,0:T(8,128)(2,1)S(1)}, u32[]{:S(2)}, u32[]{:S(2)}) async-start(bf16[16,12,3584]{2,1,0:T(8,128)(2,1)} %reshape.120), calls=%async_computation.2 | async-start | bytes 3670016 | tf_op jit(solution)/shard_map/all_to_all | solution.py:40
  270.8 1.8 copy-start.2
where the time goes:
time: 314 us; the launch traced here: 313 us
  waiting for transfers between devices  201 us (64%)
  local copies, waits for them, and re-layouts  41.6 us (13%)
  blocking collectives  24.4 us (8%)
  starting transfers between devices  22.9 us (7%)
  matrix products  14.2 us (5%)
  other arithmetic  8.21 us (3%)
    all_to_all x1, waiting for transfers between devices, deliver(): lax.all_to_all(copies, 'expert', split_axis=1, concat_axis=1, tiled=True)  121 us
    all_to_all x2, waiting for transfers between devices, collect(): lax.all_to_all(shard_parts.reshape(sources, capacity, feature_count), 'ex...  73.6 us
    all_to_all x1, blocking collectives, mirror_move(): lax.all_to_all(values, 'pipe', split_axis=split_dim, concat_axis=concat_d...  24.4 us
    all_to_all x2, starting transfers between devices, collect(): lax.all_to_all(shard_parts.reshape(sources, capacity, feature_count), 'ex...  11.6 us
    select_n x1, local copies, waits for them, and re-layouts, local(): jnp.where(upper_half, section_grads[:, :half_rows], section_grads[:, half...  8.52 us
    all_to_all x1, waiting for transfers between devices, mirror_move(): lax.all_to_all(values, 'pipe', split_axis=split_dim, concat_axis=concat_d...  6.6 us
    all_to_all x1, starting transfers between devices, deliver(): lax.all_to_all(copies, 'expert', split_axis=1, concat_axis=1, tiled=True)  6.55 us
  transfers between devices with their start and end apart: 4, of which 4 were waited for; matrix products, arithmetic and copies ran while one was open for 6% of the time, Pallas kernels for 0%

commit v1 on v0

--- a/solution.py
+++ b/solution.py
@@ -30,7 +30,12 @@
     stacks = slot_rows.shape[0]
     feature_count = slot_rows.shape[2]
     copies = jnp.repeat(slot_rows.reshape(stacks, experts, capacity, feature_count), SHARDS, axis=1)
-    landed = lax.all_to_all(copies, "expert", split_axis=1, concat_axis=1, tiled=True)
+    landed = jnp.concatenate(
+        lax.all_to_all(
+            jnp.stack(jnp.split(copies, lax.axis_size("expert"), axis=1)), "expert", 0, 0
+        ),
+        axis=1,
+    )
     return landed.reshape(stacks, experts * SHARDS * capacity, feature_count)
 
 

time: 314 us -> 325 us (1.035)
  local copies, waits for them, and re-layouts: 41.6 us -> 50 us
    unnamed x17 -> x26, local copies, waits for them, and re-layouts: 5.63 us -> 15.7 us
where the time goes in v1:
time: 325 us; the launch traced here: 324 us
  waiting for transfers between devices  201 us (62%)
  local copies, waits for them, and re-layouts  50 us (15%)
  blocking collectives  24.4 us (8%)
  starting transfers between devices  22.9 us (7%)
  matrix products  16.5 us (5%)
  other arithmetic  8.21 us (3%)
    all_to_all x1, waiting for transfers between devices, deliver(): lax.all_to_all(jnp.stack(jnp.split(copies, lax.axis_size('expert'), axis=...  121 us
    all_to_all x2, waiting for transfers between devices, collect(): lax.all_to_all(shard_parts.reshape(sources, capacity, feature_count), 'ex...  73.6 us
    all_to_all x1, blocking collectives, mirror_move(): lax.all_to_all(values, 'pipe', split_axis=split_dim, concat_axis=concat_d...  24.4 us
    unnamed x26, local copies, waits for them, and re-layouts  15.7 us
    all_to_all x2, starting transfers between devices, collect(): lax.all_to_all(shard_parts.reshape(sources, capacity, feature_count), 'ex...  11.6 us
    select_n x1, local copies, waits for them, and re-layouts, local(): jnp.where(upper_half, section_grads[:, :half_rows], section_grads[:, half...  8.54 us
    all_to_all x1, waiting for transfers between devices, mirror_move(): lax.all_to_all(values, 'pipe', split_axis=split_dim, concat_axis=concat_d...  6.77 us
    all_to_all x1, starting transfers between devices, deliver(): lax.all_to_all(jnp.stack(jnp.split(copies, lax.axis_size('expert'), axis=...  6.56 us
  transfers between devices with their start and end apart: 4, of which 4 were waited for; matrix products, arithmetic and copies ran while one was open for 6% of the time, Pallas kernels for 0%

profile of v1, /device:TPU:13, one launch (start us, length us, event | category | flops | bytes accessed | tf_op | source)
XLA Modules:
  0.0 324.0 jit_solution(129643829297920425)
XLA Ops:
  0.6 0.8 copy.122
  2.1 0.7 bitcast_add_fusion.2
  2.9 0.7 multiply_bitcast_fusion.1
  3.6 0.8 copy.126
  5.0 0.7 bitcast_add_fusion.1
  5.8 0.7 multiply_bitcast_fusion
  6.7 1.2 convolution_convert_fusion.4
  8.0 1.1 convolution_convert_fusion.5
  9.3 1.1 convolution_convert_fusion.6
  10.6 0.6 broadcast_in_dim.8
  11.3 0.8 fusion.37
  12.1 0.7 fusion.36
  12.8 0.8 fusion.35
  13.6 0.8 fusion.34
  14.3 0.8 fusion.33
  15.1 0.8 fusion.32
  15.8 0.7 fusion.31
  16.6 0.8 fusion.30
  17.3 0.8 fusion.29
  18.1 0.8 fusion.28
  18.9 0.8 fusion.27
  19.7 0.8 fusion.26
  20.5 0.8 fusion.25
  21.2 0.7 fusion.24
  22.0 0.8 fusion.23
  22.8 0.8 fusion.22
  23.5 6.6 %all-to-all-start = ((bf16[16,3,1,12,3584]{4,3,2,1,0:T(8,128)(2,1)}), bf16[16,3,1,12,3584]{4,3,2,1,0:T(8,128)(2,1)}, u32[]{:S(2)}, u32[]{:S(2)}) async-start(bf16[16,3,1,12,3584]{4,3,2,1,0:T(8,128)(2,1)} %fusion.22), calls=%async_computation | async-start | bytes 11010048 | tf_op jit(solution)/shard_map/all_to_all | solution.py:34
  30.1 120.6 %all-to-all-done = bf16[16,3,1,12,3584]{4,3,2,1,0:T(8,128)(2,1)} async-done(((bf16[16,3,1,12,3584]{4,3,2,1,0:T(8,128)(2,1)}), bf16[16,3,1,12,3584]{4,3,2,1,0:T(8,128)(2,1)}, u32[]{:S(2)}, u32[]{:S(2)}) %all-to-all-start) | async-done | bytes 4128800 | tf_op jit(solution)/shard_map/all_to_all | solution.py:34
  150.7 5.2 %fusion.56 = (bf16[1,16,1,12,3584]{4,3,2,0,1:T(8,128)(2,1)}, bf16[1,16,1,12,3584]{4,3,2,0,1:T(8,128)(2,1)}, bf16[1,16,1,12,3584]{4,3,2,0,1:T(8,128)(2,1)}) fusion(bf16[3,16,1,12,3584]{4,3,2,0,1:T(8,128)(2,1)} %bitcast.39), kind=kLoop, calls=%fused_computation.107 | loop fusion | bytes 8257536 | tf_op jit(solution)/shard_map/slice | solution.py:107
  155.8 2.4 squeeze.40
  158.3 0.5 fusion.18
  158.8 0.5 fusion.12
  159.3 3.4 %squeeze.39 = bf16[192,3584]{1,0:T(8,128)(2,1)} reshape(bf16[1,16,1,12,3584]{4,3,2,0,1:T(8,128)(2,1)} %get-tuple-element.34) | data formatting | bytes 2752512 | tf_op jit(solution)/shard_map/squeeze | solution.py:107
  162.8 2.0 fusion.3
  164.8 2.1 multiply_convert_fusion.1
  166.9 0.7 fusion.2
  167.6 0.7 fusion.1
  168.3 0.3 pad_maximum_fusion
  168.8 8.5 %copy.146 = bf16[3,1792,128]{2,0,1:T(4,128)(2,1)S(1)} copy(bf16[3,1792,128]{2,1,0:T(8,128)(2,1)S(1)} %broadcast_select_fusion) | data formatting | bytes 2752512 | tf_op jit(solution)/shard_map/jit(_where)/select_n | solution.py:139
  177.4 24.4 %all_to_all.39 = bf16[3,1792,128]{2,0,1:T(4,128)(2,1)S(1)} all-to-all(bf16[3,1792,128]{2,0,1:T(4,128)(2,1)S(1)} %copy.146), channel_id=1, replica_groups=mesh['pipe'=2,'expert'=16] {'pipe'}, dimensions={1} | all-to-all | bytes 2752512 | tf_op jit(solution)/shard_map/all_to_all | solution.py:60
  202.0 1.2 reverse.3
  203.2 2.5 copy.148
  205.7 4.8 %all-to-all-start.4 = ((bf16[6,896,128]{2,1,0:T(8,128)(2,1)}), bf16[6,896,128]{2,1,0:T(8,128)(2,1)}, u32[]{:S(2)}, u32[]{:S(2)}) async-start(bf16[6,896,128]{2,1,0:T(8,128)(2,1)} %bitcast.52), calls=%async_computation.4 | async-start | bytes 2752512 | tf_op jit(solution)/shard_map/all_to_all | solution.py:60
  210.5 2.4 squeeze.35
  212.9 0.5 fusion.20
  213.4 3.2 convolution_convert_fusion
  216.6 3.3 %reshape.120 = bf16[16,12,3584]{2,1,0:T(8,128)(2,1)} reshape(bf16[192,3584]{1,0:T(8,128)(2,1)} %convolution_convert_fusion) | data formatting | bytes 2752512 | tf_op jit(solution)/shard_map/reshape | solution.py:46
  219.9 6.8 %all-to-all-done.4 = bf16[6,896,128]{2,1,0:T(8,128)(2,1)} async-done(((bf16[6,896,128]{2,1,0:T(8,128)(2,1)}), bf16[6,896,128]{2,1,0:T(8,128)(2,1)}, u32[]{:S(2)}, u32[]{:S(2)}) %all-to-all-start.4) | async-done | bytes 1376288 | tf_op jit(solution)/shard_map/all_to_all | solution.py:60
  226.6 6.7 %all-to-all-start.1 = ((bf16[16,12,3584]{2,1,0:T(8,128)(2,1)}), bf16[16,12,3584]{2,1,0:T(8,128)(2,1)}, u32[]{:S(2)}, u32[]{:S(2)}) async-start(bf16[16,12,3584]{2,1,0:T(8,128)(2,1)} %reshape.120), calls=%async_computation.1 | async-start | bytes 3670016 | tf_op jit(solution)/shard_map/all_to_all | solution.py:45
  233.3 0.5 fusion.16
  233.9 0.5 fusion
  234.4 1.4 reshape.123
  235.8 39.4 %all-to-all-done.1 = bf16[16,12,3584]{2,1,0:T(8,128)(2,1)} async-done(((bf16[16,12,3584]{2,1,0:T(8,128)(2,1)}), bf16[16,12,3584]{2,1,0:T(8,128)(2,1)}, u32[]{:S(2)}, u32[]{:S(2)}) %all-to-all-start.1) | async-done | bytes 1376288 | tf_op jit(solution)/shard_map/all_to_all | solution.py:45
  275.2 4.9 %all-to-all-start.2 = ((bf16[16,12,3584]{2,1,0:T(8,128)(2,1)}), bf16[16,12,3584]{2,1,0:T(8,128)(2,1)S(1)}, u32[]{:S(2)}, u32[]{:S(2)}) async-start(bf16[16,12,3584]{2,1,0:T(8,128)(2,1)} %reshape.123), calls=%async_computation.2 | async-start | bytes 3670016 | tf_op jit(solution)/shard_map/all_to_all | solution.py:45
  280.2 1.5 convert_bitcast_fusion
  281.9 1.6 copy-done.2
  283.5 0.4 fusion.6
  283.9 1.0 slice_bitcast_fusion
  284.9 1.0 copy.150
  285.9 1.8 bitcast_reduce_fusion.1
  287.8 34.2 %all-to-all-done.2 = bf16[16,12,3584]{2,1,0:T(8,128)(2,1)S(1)} async-done(((bf16[16,12,3584]{2,1,0:T(8,128)(2,1)}), bf16[16,12,3584]{2,1,0:T(8,128)(2,1)S(1)}, u32[]{:S(2)}, u32[]{:S(2)}) %all-to-all-start.2) | async-done | bytes 1376288 | tf_op jit(solution)/shard_map/all_to_all | solution.py:45
  322.0 0.3 bitcast_reduce_fusion
  322.3 0.8 fusion.5
  323.1 0.9 fusion.4
  (35 shorter events, 2.7 us)
Async XLA Ops:
  0.6 158.2 %copy-start = (bf16[1,3584,128]{2,1,0:T(8,128)(2,1)S(1)}, bf16[1,3584,128]{2,1,0:T(8,128)(2,1)}, u32[]{:S(2)}) copy-start(bf16[1,3584,128]{2,1,0:T(8,128)(2,1)} %param.18) | copy-start | bytes 2752516
  23.5 127.1 %all-to-all-start = ((bf16[16,3,1,12,3584]{4,3,2,1,0:T(8,128)(2,1)}), bf16[16,3,1,12,3584]{4,3,2,1,0:T(8,128)(2,1)}, u32[]{:S(2)}, u32[]{:S(2)}) async-start(bf16[16,3,1,12,3584]{4,3,2,1,0:T(8,128)(2,1)} %fusion.22), calls=%async_computation | async-start | bytes 11010048 | tf_op jit(solution)/shard_map/all_to_all | solution.py:34
  155.8 2.5 copy-start.3
  168.7 8.7 %copy-start.1 = (bf16[3,3584,128]{2,1,0:T(8,128)(2,1)}, bf16[3,3584,128]{2,1,0:T(8,128)(2,1)S(1)}, u32[]{:S(2)}) copy-start(bf16[3,3584,128]{2,1,0:T(8,128)(2,1)S(1)} %pad_maximum_fusion) | copy-start | bytes 8257540
  205.7 20.9 %all-to-all-start.4 = ((bf16[6,896,128]{2,1,0:T(8,128)(2,1)}), bf16[6,896,128]{2,1,0:T(8,128)(2,1)}, u32[]{:S(2)}, u32[]{:S(2)}) async-start(bf16[6,896,128]{2,1,0:T(8,128)(2,1)} %bitcast.52), calls=%async_computation.4 | async-start | bytes 2752512 | tf_op jit(solution)/shard_map/all_to_all | solution.py:60
  226.6 48.6 %all-to-all-start.1 = ((bf16[16,12,3584]{2,1,0:T(8,128)(2,1)}), bf16[16,12,3584]{2,1,0:T(8,128)(2,1)}, u32[]{:S(2)}, u32[]{:S(2)}) async-start(bf16[16,12,3584]{2,1,0:T(8,128)(2,1)} %reshape.120), calls=%async_computation.1 | async-start | bytes 3670016 | tf_op jit(solution)/shard_map/all_to_all | solution.py:45
  275.2 46.7 %all-to-all-start.2 = ((bf16[16,12,3584]{2,1,0:T(8,128)(2,1)}), bf16[16,12,3584]{2,1,0:T(8,128)(2,1)S(1)}, u32[]{:S(2)}, u32[]{:S(2)}) async-start(bf16[16,12,3584]{2,1,0:T(8,128)(2,1)} %reshape.123), calls=%async_computation.2 | async-start | bytes 3670016 | tf_op jit(solution)/shard_map/all_to_all | solution.py:45
  281.7 1.8 copy-start.2
